TPU v7x, 32 devices: a whole 2x2x4 slice. The times are simulated.
32 devices in a mesh: rows: 8 (over z, x), chan: 4 (over y, core).
Axes of the slice: x: 2, y: 2, z: 4, core: 2. Of those that a mesh axis runs over, the one named last changes fastest.
Arguments:
- frames: bfloat16 [9, 32, 480, 256], P(None, 'rows', 'chan'), may hold values from -450 to 450
- spatial_weight: bfloat16 [256, 2304], P('rows'), may hold values from -0.125 to 0.125
- temporal_weight: bfloat16 [256, 768], P('rows'), may hold values from -0.21875 to 0.21875
- down_weight: bfloat16 [256, 2304], P('rows'), may hold values from -0.125 to 0.125
- norm_gain: float32 [256], replicated, may hold values from 0.5 to 1.5
- norm_shift: float32 [256], replicated, may hold values from -3 to 3
- down_bias: float32 [256], replicated, may hold values from -3 to 3
Outputs:
- latent: bfloat16 [9, 16, 240, 256], P(None, 'rows', 'chan')
All inputs are finite; a program needn't handle non-finite values.
Results may differ from a plain program's by a relative error of at most 0.0053.
Values may be sent and summed in bfloat16 or wider, within the bound.
No kernel may reach another device: no remote copies, remote signals or barrier semaphores. Data moves between devices by JAX's collectives and lax.ppermute only.
A program may use at most 128 MiB of HBM per device.

v0:
```python
import jax
import jax.numpy as jnp
from jax import lax
from jax.sharding import PartitionSpec as P

GROUPS = 32
epsilon = 1e-06


def extended_2(cells, sides, width):
    for axis, dim in sides:
        count = lax.axis_size(axis)
        ends = count - 1
        head = lax.slice_in_dim(cells, 0, width, axis=dim)
        tail = lax.slice_in_dim(cells, cells.shape[dim] - width, cells.shape[dim], axis=dim)
        cells = jnp.concatenate(
            [
                lax.ppermute(tail, axis, [(i, (i + 1) % count) for i in range(ends)]),
                cells,
                lax.ppermute(head, axis, [((i + 1) % count, i) for i in range(ends)]),
            ],
            axis=dim,
        )
    return cells


def passed_along(block, axis, distance):
    devices = range(lax.axis_size(axis))
    route = [(i - distance, i) for i in devices if i - distance in devices]
    return lax.ppermute(block, axis, route)


def spatial_taps(padded, weight_rows, width_out):
    rows_out = padded.shape[1] - 2
    cols_out = padded.shape[2] - 2
    summed = None
    for tap_index in range(9):
        row_offset = tap_index // 3
        col_offset = tap_index % 3
        window = padded[
            :, row_offset : row_offset + rows_out, col_offset : col_offset + cols_out, :
        ]
        weight_panel = weight_rows[:, tap_index * width_out : (tap_index + 1) * width_out]
        product = jnp.einsum(
            "fijc,co->fijo", window, weight_panel, preferred_element_type=jnp.float32
        )
        summed = product if summed is None else summed + product
    return summed


def temporal_taps(values, weight_rows, width_out):
    frame_count = values.shape[0]
    summed = None
    for tap_index in range(3):
        lag_frames = 2 - tap_index
        if lag_frames > 0:
            delayed = jnp.concatenate(
                [jnp.repeat(values[:1], lag_frames, axis=0), values[: frame_count - lag_frames]],
                axis=0,
            )
        else:
            delayed = values
        weight_panel = weight_rows[:, tap_index * width_out : (tap_index + 1) * width_out]
        product = jnp.einsum(
            "fijc,co->fijo", delayed, weight_panel, preferred_element_type=jnp.float32
        )
        summed = product if summed is None else summed + product
    return summed


def down_taps(extended, weight_rows, width_out):
    rows_out = (extended.shape[1] - 1) // 2
    cols_out = (extended.shape[2] - 1) // 2
    summed = None
    for tap_index in range(9):
        row_offset = tap_index // 3
        col_offset = tap_index % 3
        window = extended[
            :,
            row_offset : row_offset + 2 * rows_out : 2,
            col_offset : col_offset + 2 * cols_out : 2,
            :,
        ]
        weight_panel = weight_rows[:, tap_index * width_out : (tap_index + 1) * width_out]
        product = jnp.einsum(
            "fijc,co->fijo", window, weight_panel, preferred_element_type=jnp.float32
        )
        summed = product if summed is None else summed + product
    return summed


def group_reduce(partial_sums):
    return lax.psum(partial_sums, ("rows", "chan"))


def place_groups(channel_sums, group_width):
    local_sums = channel_sums.reshape(-1, group_width).sum(axis=1)
    return local_sums


def channel_values(group_vector, group_width):
    return jnp.repeat(group_vector, group_width)


def per_device(
    frames, spatial_weight, temporal_weight, down_weight, norm_gain, norm_shift, down_bias
):
    full_spatial, full_temporal, full_down = (
        lax.all_gather(spatial_weight, "rows", axis=0, tiled=True),
        lax.all_gather(temporal_weight, "rows", axis=0, tiled=True),
        lax.all_gather(down_weight, "rows", axis=0, tiled=True),
    )
    channels = full_spatial.shape[0]
    group_width = channels // GROUPS
    frame_count = frames.shape[0]
    rows_dev = frames.shape[1]
    width_all = frames.shape[2] * lax.axis_size("chan")
    cell_count = float(frame_count * rows_dev * lax.axis_size("rows") * width_all * group_width)
    padded = extended_2(frames, (("rows", 1), ("chan", 2)), 1)
    first = spatial_taps(padded, full_spatial, channels).astype(jnp.bfloat16)
    hidden = temporal_taps(first, full_temporal, channels)
    channel_sums = jnp.sum(hidden, axis=(0, 1, 2))
    totals = group_reduce(place_groups(channel_sums, group_width)[None])
    means = totals[0] / cell_count
    chan_mean = channel_values(means, group_width)
    centered = hidden - chan_mean
    spread = group_reduce(
        place_groups(jnp.sum(centered * centered, axis=(0, 1, 2)), group_width)[None]
    )
    variance = spread[0] / cell_count
    chan_var = channel_values(variance, group_width)
    act = jax.nn.silu(centered * lax.rsqrt(chan_var + epsilon) * norm_gain + norm_shift).astype(
        jnp.bfloat16
    )
    below = passed_along(act[:, :1], "rows", -1)
    extended = jnp.concatenate([act, below], axis=1)
    beside = passed_along(extended[:, :, :1], "chan", -1)
    extended = jnp.concatenate([extended, beside], axis=2)
    latent = down_taps(extended, full_down, channels) + down_bias
    return latent.astype(jnp.bfloat16)


def solution(mesh):
    placed = (
        P(None, "rows", "chan", None),
        P("rows", None),
        P("rows", None),
        P("rows", None),
        P(),
        P(),
        P(),
    )
    return jax.shard_map(
        per_device,
        mesh=mesh,
        in_specs=placed,
        out_specs=P(None, "rows", "chan", None),
        check_vma=False,
    )
```

profile of v0, /device:TPU:3, one launch (start us, length us, event | category | flops | bytes accessed | tf_op | source)
XLA Modules:
  0.0 319.5 jit_solution(4577024968184721207)
XLA Ops:
  7.3 2.1 fusion.64
  9.4 3.2 collective-permute-start
  12.6 2.9 collective-permute-start.1
  15.5 22.7 %collective-permute-done = bf16[9,1,120,256]{3,2,1,0:T(8,128)(2,1)} collective-permute-done((bf16[9,1,120,256]{3,2,1,0:T(8,128)(2,1)S(1)}, bf16[9,1,120,256]{3,2,1,0:T(8,128)(2,1)}, u32[]{:S(2)}, u32[]{:S(2)}) %collective-permute-start) | collective-permute-done | bytes 552992 | tf_op jit(solution)/shard_map/ppermute | solution.py:18
  42.3 4.6 %collective-permute-start.2 = (bf16[9,6,1,256]{3,2,1,0:T(2,128)(2,1)S(1)}, bf16[9,6,1,256]{3,2,1,0:T(2,128)(2,1)S(1)}, u32[]{:S(2)}, u32[]{:S(2)}) collective-permute-start(bf16[9,6,1,256]{3,2,1,0:T(2,128)(2,1)S(1)} %get-tuple-element.6), channel_id=1, source_target_pairs={{0,1},{1,2},{2,3},{4,5},{5,6},{6,7},{8,9},{9,10},{10,11},{12,13},{... | collective-permute-start | bytes 82952 | tf_op jit(solution)/shard_map/ppermute | solution.py:18
  46.9 25.9 %all_gather.10 = bf16[256,768]{1,0:T(8,128)(2,1)} all-gather(bf16[32,768]{1,0:T(8,128)(2,1)S(1)} %copy-done.12), channel_id=1, replica_groups=mesh['rows'=8,'chan'=4] {'rows'}, dimensions={0}, use_global_device_ids=true | all-gather | bytes 442368 | tf_op jit(solution)/shard_map/all_gather | solution.py:110
  72.8 5.5 %collective-permute-start.3 = (bf16[9,6,1,256]{3,2,1,0:T(2,128)(2,1)S(1)}, bf16[9,6,1,256]{3,2,1,0:T(2,128)(2,1)S(1)}, u32[]{:S(2)}, u32[]{:S(2)}) collective-permute-start(bf16[9,6,1,256]{3,2,1,0:T(2,128)(2,1)S(1)} %get-tuple-element.5), channel_id=1, source_target_pairs={{1,0},{2,1},{3,2},{5,4},{6,5},{7,6},{9,8},{10,9},{11,10},{13,12},{... | collective-permute-start | bytes 82952 | tf_op jit(solution)/shard_map/ppermute | solution.py:20
  78.4 3.8 %fusion.15 = f32[9,4,120,256]{3,2,1,0:T(8,128)} fusion(bf16[9,6,120,256]{3,2,1,0:T(8,128)(2,1)S(1)} %constant_dynamic-update-slice_fusion, bf16[9,6,1,256]{3,2,1,0:T(2,128)(2,1)S(1)} %collective-permute-done.2, bf16[256,2304]{1,0:T(8,128)(2,1)} %all-gather.3.cloned.1.call-done), kind=kOutput, calls=%fused_computation.29 | convolution fusion | flops 570654720 | bytes 7900160 | tf_op jit(solution)/shard_map/fijc,co->fijo/dot_general | solution.py:44
  82.2 2.9 fusion.18
  85.1 2.8 fusion.12
  87.8 2.9 fusion.9
  90.8 2.9 fusion.22
  93.6 3.9 %fusion = f32[9,4,120,256]{3,2,1,0:T(8,128)} fusion(bf16[9,4,120,256]{3,2,1,0:T(8,128)(2,1)S(1)} %copy-done, bf16[9,1,120,256]{3,2,1,0:T(8,128)(2,1)} %collective-permute-done, bf16[256,2304]{1,0:T(8,128)(2,1)S(1)} %copy-done.11), kind=kOutput, calls=%fused_computation.15 | convolution fusion | flops 571760640 | bytes 7319552 | tf_op jit(solution)/shard_map/fijc,co->fijo/dot_general | solution.py:44
  99.3 2.9 fusion.50
  102.2 12.6 %add_convert_fusion = bf16[9,4,120,256]{3,2,1,0:T(8,128)(2,1)} fusion(f32[9,4,120,256]{3,2,1,0:T(8,128)S(1)} %fusion.4, f32[9,4,120,256]{3,2,1,0:T(8,128)} %fusion.22, f32[9,4,120,256]{3,2,1,0:T(8,128)} %fusion.9, f32[9,4,120,256]{3,2,1,0:T(8,128)} %fusion.50, f32[9,4,120,256]{3,2,1,0:T(8,128)} %fusion.15, f32[9,4,120,256]{3,2,1,0:T(8,128)} %fusion.12, ...), kind=kOutput, calls=%fused_computation.7 | convolution fusion | flops 580608000 | bytes 41105408 | tf_op jit(solution)/shard_map/fijc,co->fijo/dot_general | solution.py:44
  120.4 3.0 fusion.65
  123.7 38.6 %psum.14 = f32[1,32]{1,0:T(1,128)S(1)} all-reduce(f32[1,32]{1,0:T(1,128)S(1)} %bitcast.127), channel_id=1, replica_groups=mesh['rows'=8,'chan'=4] {'rows','chan'}, use_global_device_ids=true, to_apply=%region_2.0 | all-reduce | flops 32 | bytes 256 | tf_op jit(solution)/shard_map/psum | solution.py:93
  162.5 2.9 multiply_reduce_fusion
  165.5 41.8 %psum.15 = f32[1,32]{1,0:T(1,128)S(1)} all-reduce(f32[1,32]{1,0:T(1,128)S(1)} %bitcast.126), channel_id=1, replica_groups=mesh['rows'=8,'chan'=4] {'rows','chan'}, use_global_device_ids=true, to_apply=%region_5.0 | all-reduce | flops 32 | bytes 256 | tf_op jit(solution)/shard_map/psum | solution.py:93
  207.5 3.6 %multiply_convert_fusion = bf16[9,4,120,256]{3,2,1,0:T(8,128)(2,1)S(1)} fusion(f32[9,4,120,256]{3,2,1,0:T(8,128)} %get-tuple-element.12, f32[256]{0:T(256)S(1)} %copy-done.13, f32[256]{0:T(256)S(1)} %copy-done.14, f32[256]{0:T(256)S(1)} %rsqrt.16, f32[256]{0:T(256)S(1)} %sub.10), kind=kLoop, calls=%fused_computation.4 | loop fusion | flops 9953280 | bytes 6639616 | tf_op jit(solution)/shard_map/convert_element_type | solution.py:132
  214.8 2.2 fusion.48
  217.1 10.4 %collective-permute-done.4 = bf16[9,1,120,256]{3,2,1,0:T(8,128)(2,1)S(1)} collective-permute-done((bf16[9,1,120,256]{3,2,1,0:T(8,128)(2,1)}, bf16[9,1,120,256]{3,2,1,0:T(8,128)(2,1)S(1)}, u32[]{:S(2)}, u32[]{:S(2)}) %collective-permute-start.4) | collective-permute-done | bytes 552992 | tf_op jit(solution)/shard_map/ppermute | solution.py:30
  229.3 10.3 %slice.188 = bf16[9,2,60,256]{3,2,1,0:T(8,128)(2,1)} slice(bf16[9,5,120,256]{3,2,1,0:T(8,128)(2,1)} %pad_maximum_fusion), slice={[0:9:1], [1:5:2], [0:120:2], [0:256:1]} | slice | bytes 1105920 | tf_op jit(solution)/shard_map/slice | solution.py:78
  239.6 8.5 %slice.194 = bf16[9,2,60,256]{3,2,1,0:T(8,128)(2,1)S(1)} slice(bf16[9,5,120,256]{3,2,1,0:T(8,128)(2,1)} %pad_maximum_fusion), slice={[0:9:1], [2:5:2], [0:120:2], [0:256:1]} | slice | bytes 1105920 | tf_op jit(solution)/shard_map/slice | solution.py:78
  248.2 4.5 %collective-permute-start.5 = (bf16[9,5,1,256]{3,2,1,0:T(2,128)(2,1)S(1)}, bf16[9,5,1,256]{3,2,1,0:T(2,128)(2,1)S(1)}, u32[]{:S(2)}, u32[]{:S(2)}) collective-permute-start(bf16[9,5,1,256]{3,2,1,0:T(2,128)(2,1)S(1)} %fusion.51), channel_id=1, source_target_pairs={{1,0},{2,1},{3,2},{5,4},{6,5},{7,6},{9,8},{10,9},{11,10},{13,12},{... | collective-permute-start | bytes 69128 | tf_op jit(solution)/shard_map/ppermute | solution.py:30
  252.7 2.3 fusion.47
  254.9 2.2 fusion.44
  259.2 10.5 %slice.184 = bf16[9,2,60,256]{3,2,1,0:T(8,128)(2,1)} slice(bf16[9,5,121,256]{3,2,1,0:T(8,128)(2,1)} %pad_maximum_fusion.1), slice={[0:9:1], [0:4:2], [1:121:2], [0:256:1]} | slice | bytes 1105920 | tf_op jit(solution)/shard_map/slice | solution.py:78
  269.6 10.2 %slice.198 = bf16[9,2,60,256]{3,2,1,0:T(8,128)(2,1)} slice(bf16[9,5,121,256]{3,2,1,0:T(8,128)(2,1)} %pad_maximum_fusion.1), slice={[0:9:1], [2:5:2], [2:121:2], [0:256:1]} | slice | bytes 1105920 | tf_op jit(solution)/shard_map/slice | solution.py:78
  279.8 10.1 %slice.196 = bf16[9,2,60,256]{3,2,1,0:T(8,128)(2,1)} slice(bf16[9,5,121,256]{3,2,1,0:T(8,128)(2,1)} %pad_maximum_fusion.1), slice={[0:9:1], [2:5:2], [1:121:2], [0:256:1]} | slice | bytes 1105920 | tf_op jit(solution)/shard_map/slice | solution.py:78
  289.9 6.0 %slice.192 = bf16[9,2,60,256]{3,2,1,0:T(8,128)(2,1)} slice(bf16[9,5,121,256]{3,2,1,0:T(8,128)(2,1)S(1)} %copy-done.2), slice={[0:9:1], [1:5:2], [2:121:2], [0:256:1]} | slice | bytes 1105920 | tf_op jit(solution)/shard_map/slice | solution.py:78
  295.9 5.9 %slice.190 = bf16[9,2,60,256]{3,2,1,0:T(8,128)(2,1)} slice(bf16[9,5,121,256]{3,2,1,0:T(8,128)(2,1)S(1)} %copy-done.2), slice={[0:9:1], [1:5:2], [1:121:2], [0:256:1]} | slice | bytes 1105920 | tf_op jit(solution)/shard_map/slice | solution.py:78
  (79 shorter events, 31.2 us)
Async XLA Ops:
  6.5 71.8 %all-gather.3.cloned.1.call-start = ((), (), s32[]{:S(2)}) async-start(), calls=%async_computation | async-start | bytes 1327104 | tf_op jit(solution)/shard_map/all_gather | solution.py:109
  7.3 207.6 %all-gather.5.cloned.1.call-start = ((), (), s32[]{:S(2)}) async-start(), calls=%async_computation.1 | async-start | bytes 1327104 | tf_op jit(solution)/shard_map/all_gather | solution.py:111
  9.4 28.8 %collective-permute-start = (bf16[9,1,120,256]{3,2,1,0:T(8,128)(2,1)S(1)}, bf16[9,1,120,256]{3,2,1,0:T(8,128)(2,1)}, u32[]{:S(2)}, u32[]{:S(2)}) collective-permute-start(bf16[9,1,120,256]{3,2,1,0:T(8,128)(2,1)S(1)} %get-tuple-element.9), channel_id=1, source_target_pairs={{0,4},{4,8},{8,12},{12,16},{16,20},{20,24},{24,28},{1,5},{5,9},{9,... | collective-permute-start | bytes 1658888 | tf_op jit(solution)/shard_map/ppermute | solution.py:18
  12.6 28.5 %collective-permute-start.1 = (bf16[9,1,120,256]{3,2,1,0:T(8,128)(2,1)}, bf16[9,1,120,256]{3,2,1,0:T(8,128)(2,1)}, u32[]{:S(2)}, u32[]{:S(2)}) collective-permute-start(bf16[9,1,120,256]{3,2,1,0:T(8,128)(2,1)} %get-tuple-element.10), channel_id=1, source_target_pairs={{4,0},{8,4},{12,8},{16,12},{20,16},{24,20},{28,24},{5,1},{9,5},{13... | collective-permute-start | bytes 1658888 | tf_op jit(solution)/shard_map/ppermute | solution.py:20
  39.3 7.6 %copy-start.12 = (bf16[32,768]{1,0:T(8,128)(2,1)S(1)}, bf16[32,768]{1,0:T(8,128)(2,1)}, u32[]{:S(2)}) copy-start(bf16[32,768]{1,0:T(8,128)(2,1)} %param.9) | copy-start | bytes 147460
  42.3 36.0 %collective-permute-start.2 = (bf16[9,6,1,256]{3,2,1,0:T(2,128)(2,1)S(1)}, bf16[9,6,1,256]{3,2,1,0:T(2,128)(2,1)S(1)}, u32[]{:S(2)}, u32[]{:S(2)}) collective-permute-start(bf16[9,6,1,256]{3,2,1,0:T(2,128)(2,1)S(1)} %get-tuple-element.6), channel_id=1, source_target_pairs={{0,1},{1,2},{2,3},{4,5},{5,6},{6,7},{8,9},{9,10},{10,11},{12,13},{... | collective-permute-start | bytes 82952 | tf_op jit(solution)/shard_map/ppermute | solution.py:18
  72.8 12.3 %collective-permute-start.3 = (bf16[9,6,1,256]{3,2,1,0:T(2,128)(2,1)S(1)}, bf16[9,6,1,256]{3,2,1,0:T(2,128)(2,1)S(1)}, u32[]{:S(2)}, u32[]{:S(2)}) collective-permute-start(bf16[9,6,1,256]{3,2,1,0:T(2,128)(2,1)S(1)} %get-tuple-element.5), channel_id=1, source_target_pairs={{1,0},{2,1},{3,2},{5,4},{6,5},{7,6},{9,8},{10,9},{11,10},{13,12},{... | collective-permute-start | bytes 82952 | tf_op jit(solution)/shard_map/ppermute | solution.py:20
  78.4 3.8 %copy-start.11 = (bf16[256,2304]{1,0:T(8,128)(2,1)S(1)}, bf16[256,2304]{1,0:T(8,128)(2,1)}, u32[]{:S(2)}) copy-start(bf16[256,2304]{1,0:T(8,128)(2,1)} %all-gather.3.cloned.1.call-done) | copy-start | bytes 3538948
  90.8 2.9 copy-start
  114.8 1.6 copy-start.1
  116.4 1.0 copy-start.10
  117.4 1.5 slice-start
  118.9 1.5 slice-start.1
  123.5 84.1 %copy-start.13 = (f32[256]{0:T(256)S(1)}, f32[256]{0:T(256)}, u32[]{:S(2)}) copy-start(f32[256]{0:T(256)} %param.12) | copy-start | bytes 3076
  123.5 84.1 %copy-start.14 = (f32[256]{0:T(256)S(1)}, f32[256]{0:T(256)}, u32[]{:S(2)}) copy-start(f32[256]{0:T(256)} %param.11) | copy-start | bytes 3076
  212.0 15.5 %collective-permute-start.4 = (bf16[9,1,120,256]{3,2,1,0:T(8,128)(2,1)}, bf16[9,1,120,256]{3,2,1,0:T(8,128)(2,1)S(1)}, u32[]{:S(2)}, u32[]{:S(2)}) collective-permute-start(bf16[9,1,120,256]{3,2,1,0:T(8,128)(2,1)} %slice.226), channel_id=1, source_target_pairs={{4,0},{8,4},{12,8},{16,12},{20,16},{24,20},{28,24},{5,1},{9,5},{13... | collective-permute-start | bytes 1658888 | tf_op jit(solution)/shard_map/ppermute | solution.py:30
  248.1 4.6 %copy-start.8 = (bf16[9,2,60,256]{3,2,1,0:T(8,128)(2,1)S(1)}, bf16[9,2,60,256]{3,2,1,0:T(8,128)(2,1)}, u32[]{:S(2)}) copy-start(bf16[9,2,60,256]{3,2,1,0:T(8,128)(2,1)} %slice.188) | copy-start | bytes 1658884
  248.2 9.0 %collective-permute-start.5 = (bf16[9,5,1,256]{3,2,1,0:T(2,128)(2,1)S(1)}, bf16[9,5,1,256]{3,2,1,0:T(2,128)(2,1)S(1)}, u32[]{:S(2)}, u32[]{:S(2)}) collective-permute-start(bf16[9,5,1,256]{3,2,1,0:T(2,128)(2,1)S(1)} %fusion.51), channel_id=1, source_target_pairs={{1,0},{2,1},{3,2},{5,4},{6,5},{7,6},{9,8},{10,9},{11,10},{13,12},{... | collective-permute-start | bytes 69128 | tf_op jit(solution)/shard_map/ppermute | solution.py:30
  259.2 30.7 %copy-start.2 = (bf16[9,5,121,256]{3,2,1,0:T(8,128)(2,1)S(1)}, bf16[9,5,121,256]{3,2,1,0:T(8,128)(2,1)}, u32[]{:S(2)}) copy-start(bf16[9,5,121,256]{3,2,1,0:T(8,128)(2,1)} %pad_maximum_fusion.1) | copy-start | bytes 8363524
  302.8 3.1 copy-start.9
  302.8 4.3 %copy-start.7 = (bf16[9,2,60,256]{3,2,1,0:T(8,128)(2,1)S(1)}, bf16[9,2,60,256]{3,2,1,0:T(8,128)(2,1)}, u32[]{:S(2)}) copy-start(bf16[9,2,60,256]{3,2,1,0:T(8,128)(2,1)} %slice.190) | copy-start | bytes 1658884
  304.3 4.2 %copy-start.5 = (f32[9,2,60,256]{3,2,1,0:T(8,128)S(1)}, f32[9,2,60,256]{3,2,1,0:T(8,128)}, u32[]{:S(2)}) copy-start(f32[9,2,60,256]{3,2,1,0:T(8,128)} %fusion.48) | copy-start | bytes 3317764
  304.3 4.2 %copy-start.6 = (bf16[9,2,60,256]{3,2,1,0:T(8,128)(2,1)S(1)}, bf16[9,2,60,256]{3,2,1,0:T(8,128)(2,1)}, u32[]{:S(2)}) copy-start(bf16[9,2,60,256]{3,2,1,0:T(8,128)(2,1)} %slice.184) | copy-start | bytes 1658884
  307.1 2.6 copy-start.3
  307.1 2.6 copy-start.4
  307.1 2.6 copy-start.15
Sparse Core Ops, SparseCore 0:
  9.5 52.3 all-gather.2
  64.2 39.7 all-gather.4
where the time goes:
time: 322 us; the launch traced here: 320 us
  blocking collectives  106 us (33%)
  local copies, waits for them, and re-layouts  76.4 us (24%)
  matrix products  56 us (17%)
  waiting for transfers between devices  33.9 us (11%)
  starting transfers between devices  22.6 us (7%)
  between operations  13.8 us (4%)
  other arithmetic  10.5 us (3%)
    psum x2, blocking collectives, group_reduce(): return lax.psum(partial_sums, ('rows', 'chan'))  80.4 us
    slice x9, local copies, waits for them, and re-layouts, down_taps(): extended[:, row_offset:row_offset + 2 * rows_out:2, col_offset:col_offset...  63.3 us
    dot_general x9, matrix products, spatial_taps(): jnp.einsum('fijc,co->fijo', window, weight_panel, preferred_element_type=...  36.4 us
    all_gather x1, blocking collectives, per_device(): lax.all_gather(temporal_weight, 'rows', axis=0, tiled=True)  25.9 us
    ppermute x2, waiting for transfers between devices, extended_2(): lax.ppermute(tail, axis, [(i, (i + 1) % count) for i in range(ends)])  22.7 us
    dot_general x9, matrix products, down_taps(): jnp.einsum('fijc,co->fijo', window, weight_panel, preferred_element_type=...  15.1 us
    ppermute x2, waiting for transfers between devices, passed_along(): return lax.ppermute(block, axis, route)  10.4 us
    ppermute x2, starting transfers between devices, extended_2(): lax.ppermute(head, axis, [((i + 1) % count, i) for i in range(ends)])  8.43 us
  transfers between devices with their start and end apart: 8, of which 2 were waited for; matrix products, arithmetic and copies ran while one was open for 20% of the time, Pallas kernels for 0%

commit v1 on v0

--- a/solution.py
+++ b/solution.py
@@ -1,3 +1,4 @@
+import functools
 import jax
 import jax.numpy as jnp
 from jax import lax
@@ -5,6 +6,13 @@
 
 GROUPS = 32
 epsilon = 1e-06
+
+
+def _prepare_kinds(point, bus_axis, net_axis):
+    return lax.psum(lax.psum(point, bus_axis), net_axis)
+
+
+_raise_blocks = functools.partial(_prepare_kinds, bus_axis="chan", net_axis="rows")
 
 
 def extended_2(cells, sides, width):
@@ -90,7 +98,7 @@
 
 
 def group_reduce(partial_sums):
-    return lax.psum(partial_sums, ("rows", "chan"))
+    return _raise_blocks(partial_sums)
 
 
 def place_groups(channel_sums, group_width):

time: 322 us -> 289 us (0.90)
  blocking collectives: 106 us -> 74.2 us
    psum x2 -> x4, blocking collectives: 80.4 us -> 48.3 us  [_prepare_kinds(): return lax.psum(lax.psum(point, bus_axis), net_axis)]
  transfers between devices with their start and end apart: 8 -> 8, of which waited for: 2 -> 2; matrix products, arithmetic and copies ran while one was open for 20% -> 22% of each run, Pallas kernels for 0% -> 0%
where the time goes in v1:
time: 289 us; the launch traced here: 287 us
  local copies, waits for them, and re-layouts  76.4 us (26%)
  blocking collectives  74.2 us (26%)
  matrix products  55.8 us (19%)
  waiting for transfers between devices  30.9 us (11%)
  starting transfers between devices  25.6 us (9%)
  between operations  13.8 us (5%)
  other arithmetic  10.5 us (4%)
    slice x9, local copies, waits for them, and re-layouts, down_taps(): extended[:, row_offset:row_offset + 2 * rows_out:2, col_offset:col_offset...  63.3 us
    psum x4, blocking collectives, _prepare_kinds(): return lax.psum(lax.psum(point, bus_axis), net_axis)  48.3 us
    dot_general x9, matrix products, spatial_taps(): jnp.einsum('fijc,co->fijo', window, weight_panel, preferred_element_type=...  36.3 us
    all_gather x1, blocking collectives, per_device(): lax.all_gather(temporal_weight, 'rows', axis=0, tiled=True)  25.9 us
    ppermute x2, waiting for transfers between devices, extended_2(): lax.ppermute(tail, axis, [(i, (i + 1) % count) for i in range(ends)])  22.7 us
    dot_general x9, matrix products, down_taps(): jnp.einsum('fijc,co->fijo', window, weight_panel, preferred_element_type=...  15.1 us
    ppermute x2, starting transfers between devices, passed_along(): return lax.ppermute(block, axis, route)  9.41 us
    ppermute x2, starting transfers between devices, extended_2(): lax.ppermute(head, axis, [((i + 1) % count, i) for i in range(ends)])  8.43 us
  transfers between devices with their start and end apart: 8, of which 2 were waited for; matrix products, arithmetic and copies ran while one was open for 22% of the time, Pallas kernels for 0%

profile of v1, /device:TPU:3, one launch (start us, length us, event | category | flops | bytes accessed | tf_op | source)
XLA Modules:
  0.0 287.2 jit_solution(919798174334945147)
XLA Ops:
  9.4 3.2 %collective-permute-start = (bf16[9,1,120,256]{3,2,1,0:T(8,128)(2,1)S(1)}, bf16[9,1,120,256]{3,2,1,0:T(8,128)(2,1)}, u32[]{:S(2)}, u32[]{:S(2)}) collective-permute-start(bf16[9,1,120,256]{3,2,1,0:T(8,128)(2,1)S(1)} %get-tuple-element.9), channel_id=1, source_target_pairs={{0,4},{4,8},{8,12},{12,16},{16,20},{20,24},{24,28},{1,5},{5,9},{9,... | collective-permute-start | bytes 1658888 | tf_op jit(solution)/shard_map/ppermute | solution.py:26
  12.6 2.9 %collective-permute-start.1 = (bf16[9,1,120,256]{3,2,1,0:T(8,128)(2,1)}, bf16[9,1,120,256]{3,2,1,0:T(8,128)(2,1)}, u32[]{:S(2)}, u32[]{:S(2)}) collective-permute-start(bf16[9,1,120,256]{3,2,1,0:T(8,128)(2,1)} %get-tuple-element.10), channel_id=1, source_target_pairs={{4,0},{8,4},{12,8},{16,12},{20,16},{24,20},{28,24},{5,1},{9,5},{13... | collective-permute-start | bytes 1658888 | tf_op jit(solution)/shard_map/ppermute | solution.py:28
  15.5 22.7 %collective-permute-done = bf16[9,1,120,256]{3,2,1,0:T(8,128)(2,1)} collective-permute-done((bf16[9,1,120,256]{3,2,1,0:T(8,128)(2,1)S(1)}, bf16[9,1,120,256]{3,2,1,0:T(8,128)(2,1)}, u32[]{:S(2)}, u32[]{:S(2)}) %collective-permute-start) | collective-permute-done | bytes 552992 | tf_op jit(solution)/shard_map/ppermute | solution.py:26
  42.3 4.6 %collective-permute-start.2 = (bf16[9,6,1,256]{3,2,1,0:T(2,128)(2,1)S(1)}, bf16[9,6,1,256]{3,2,1,0:T(2,128)(2,1)S(1)}, u32[]{:S(2)}, u32[]{:S(2)}) collective-permute-start(bf16[9,6,1,256]{3,2,1,0:T(2,128)(2,1)S(1)} %get-tuple-element.6), channel_id=1, source_target_pairs={{0,1},{1,2},{2,3},{4,5},{5,6},{6,7},{8,9},{9,10},{10,11},{12,13},{... | collective-permute-start | bytes 82952 | tf_op jit(solution)/shard_map/ppermute | solution.py:26
  46.9 25.9 %all_gather.10 = bf16[256,768]{1,0:T(8,128)(2,1)} all-gather(bf16[32,768]{1,0:T(8,128)(2,1)S(1)} %copy-done.12), channel_id=1, replica_groups=mesh['rows'=8,'chan'=4] {'rows'}, dimensions={0}, use_global_device_ids=true | all-gather | bytes 442368 | tf_op jit(solution)/shard_map/all_gather | solution.py:118
  72.8 5.5 %collective-permute-start.3 = (bf16[9,6,1,256]{3,2,1,0:T(2,128)(2,1)S(1)}, bf16[9,6,1,256]{3,2,1,0:T(2,128)(2,1)S(1)}, u32[]{:S(2)}, u32[]{:S(2)}) collective-permute-start(bf16[9,6,1,256]{3,2,1,0:T(2,128)(2,1)S(1)} %get-tuple-element.5), channel_id=1, source_target_pairs={{1,0},{2,1},{3,2},{5,4},{6,5},{7,6},{9,8},{10,9},{11,10},{13,12},{... | collective-permute-start | bytes 82952 | tf_op jit(solution)/shard_map/ppermute | solution.py:28
  78.4 3.8 %fusion.15 = f32[9,4,120,256]{3,2,1,0:T(8,128)} fusion(bf16[9,6,120,256]{3,2,1,0:T(8,128)(2,1)S(1)} %constant_dynamic-update-slice_fusion, bf16[9,6,1,256]{3,2,1,0:T(2,128)(2,1)S(1)} %collective-permute-done.2, bf16[256,2304]{1,0:T(8,128)(2,1)} %all-gather.3.cloned.1.call-done), kind=kOutput, calls=%fused_computation.29 | convolution fusion | flops 570654720 | bytes 7900160 | tf_op jit(solution)/shard_map/fijc,co->fijo/dot_general | solution.py:52
  82.2 2.8 fusion.18
  85.0 2.8 fusion.12
  87.8 2.9 %fusion.9 = f32[9,4,120,256]{3,2,1,0:T(8,128)} fusion(bf16[9,6,120,256]{3,2,1,0:T(8,128)(2,1)S(1)} %constant_dynamic-update-slice_fusion, bf16[9,6,1,256]{3,2,1,0:T(2,128)(2,1)S(1)} %collective-permute-done.3, bf16[256,2304]{1,0:T(8,128)(2,1)S(1)} %copy-done.11), kind=kOutput, calls=%fused_computation.25 | convolution fusion | flops 570654720 | bytes 7927808 | tf_op jit(solution)/shard_map/fijc,co->fijo/dot_general | solution.py:52
  90.7 2.9 fusion.22
  93.6 3.9 %fusion = f32[9,4,120,256]{3,2,1,0:T(8,128)} fusion(bf16[9,4,120,256]{3,2,1,0:T(8,128)(2,1)S(1)} %copy-done, bf16[9,1,120,256]{3,2,1,0:T(8,128)(2,1)} %collective-permute-done, bf16[256,2304]{1,0:T(8,128)(2,1)S(1)} %copy-done.11), kind=kOutput, calls=%fused_computation.15 | convolution fusion | flops 571760640 | bytes 7319552 | tf_op jit(solution)/shard_map/fijc,co->fijo/dot_general | solution.py:52
  99.2 2.9 %fusion.50 = f32[9,4,120,256]{3,2,1,0:T(8,128)} fusion(bf16[9,4,120,256]{3,2,1,0:T(8,128)(2,1)S(1)} %copy-done, bf16[256,2304]{1,0:T(8,128)(2,1)S(1)} %copy-done.11), kind=kOutput, calls=%fused_computation.81 | convolution fusion | flops 566231040 | bytes 6766592 | tf_op jit(solution)/shard_map/fijc,co->fijo/dot_general | solution.py:52
  102.1 12.6 %add_convert_fusion = bf16[9,4,120,256]{3,2,1,0:T(8,128)(2,1)} fusion(f32[9,4,120,256]{3,2,1,0:T(8,128)S(1)} %fusion.4, f32[9,4,120,256]{3,2,1,0:T(8,128)} %fusion.22, f32[9,4,120,256]{3,2,1,0:T(8,128)} %fusion.9, f32[9,4,120,256]{3,2,1,0:T(8,128)} %fusion.50, f32[9,4,120,256]{3,2,1,0:T(8,128)} %fusion.15, f32[9,4,120,256]{3,2,1,0:T(8,128)} %fusion.12, ...), kind=kOutput, calls=%fused_computation.7 | convolution fusion | flops 580608000 | bytes 41105408 | tf_op jit(solution)/shard_map/fijc,co->fijo/dot_general | solution.py:52
  120.3 3.0 %fusion.65 = (f32[256]{0:T(256)S(1)}, f32[9,4,120,256]{3,2,1,0:T(8,128)}) fusion(f32[9,4,120,256]{3,2,1,0:T(8,128)S(1)} %fusion.49, f32[9,4,120,256]{3,2,1,0:T(8,128)S(1)} %fusion.24, bf16[256,768]{1,0:T(8,128)(2,1)S(1)} %copy-done.10, bf16[8,4,120,256]{3,2,1,0:T(8,128)(2,1)S(1)} %slice-done.1, bf16[1,4,120,256]{3,2,1,0:T(8,128)(2,1)S(1)} %get-tuple-element.7), kind=kOutput, calls=%fused_computation.106 | convolution fusion | flops 570654464 | bytes 15614976 | tf_op jit(solution)/shard_map/fijc,co->fijo/dot_general | solution.py:72
  123.5 5.7 %psum.28 = f32[1,32]{1,0:T(1,128)S(1)} all-reduce(f32[1,32]{1,0:T(1,128)S(1)} %bitcast.127), channel_id=1, replica_groups=mesh['rows'=8,'chan'=4] {'chan'}, use_global_device_ids=true, to_apply=%region_2.0 | all-reduce | flops 32 | bytes 256 | tf_op jit(solution)/shard_map/psum | solution.py:12
  129.2 15.2 %psum.29 = f32[1,32]{1,0:T(1,128)S(1)} all-reduce(f32[1,32]{1,0:T(1,128)S(1)} %psum.28), channel_id=1, replica_groups=mesh['rows'=8,'chan'=4] {'rows'}, use_global_device_ids=true, to_apply=%region_3.0 | all-reduce | flops 32 | bytes 256 | tf_op jit(solution)/shard_map/psum | solution.py:12
  144.6 2.9 multiply_reduce_fusion
  147.7 10.8 %psum.30 = f32[1,32]{1,0:T(1,128)S(1)} all-reduce(f32[1,32]{1,0:T(1,128)S(1)} %bitcast.126), channel_id=1, replica_groups=mesh['rows'=8,'chan'=4] {'chan'}, use_global_device_ids=true, to_apply=%region_6.0 | all-reduce | flops 32 | bytes 256 | tf_op jit(solution)/shard_map/psum | solution.py:12
  158.4 16.6 %psum.31 = f32[1,32]{1,0:T(1,128)S(1)} all-reduce(f32[1,32]{1,0:T(1,128)S(1)} %psum.30), channel_id=1, replica_groups=mesh['rows'=8,'chan'=4] {'rows'}, use_global_device_ids=true, to_apply=%region_7.0 | all-reduce | flops 32 | bytes 256 | tf_op jit(solution)/shard_map/psum | solution.py:12
  175.3 3.6 %multiply_convert_fusion = bf16[9,4,120,256]{3,2,1,0:T(8,128)(2,1)S(1)} fusion(f32[9,4,120,256]{3,2,1,0:T(8,128)} %get-tuple-element.12, f32[256]{0:T(256)S(1)} %copy-done.13, f32[256]{0:T(256)S(1)} %copy-done.14, f32[256]{0:T(256)S(1)} %rsqrt.16, f32[256]{0:T(256)S(1)} %sub.10), kind=kLoop, calls=%fused_computation.4 | loop fusion | flops 9953280 | bytes 6639616 | tf_op jit(solution)/shard_map/convert_element_type | solution.py:140
  184.8 7.4 %collective-permute-done.4 = bf16[9,1,120,256]{3,2,1,0:T(8,128)(2,1)S(1)} collective-permute-done((bf16[9,1,120,256]{3,2,1,0:T(8,128)(2,1)}, bf16[9,1,120,256]{3,2,1,0:T(8,128)(2,1)S(1)}, u32[]{:S(2)}, u32[]{:S(2)}) %collective-permute-start.4) | collective-permute-done | bytes 552992 | tf_op jit(solution)/shard_map/ppermute | solution.py:38
  194.0 10.3 %slice.188 = bf16[9,2,60,256]{3,2,1,0:T(8,128)(2,1)} slice(bf16[9,5,120,256]{3,2,1,0:T(8,128)(2,1)} %pad_maximum_fusion), slice={[0:9:1], [1:5:2], [0:120:2], [0:256:1]} | slice | bytes 1105920 | tf_op jit(solution)/shard_map/slice | solution.py:86
  204.3 8.5 %slice.194 = bf16[9,2,60,256]{3,2,1,0:T(8,128)(2,1)S(1)} slice(bf16[9,5,120,256]{3,2,1,0:T(8,128)(2,1)} %pad_maximum_fusion), slice={[0:9:1], [2:5:2], [0:120:2], [0:256:1]} | slice | bytes 1105920 | tf_op jit(solution)/shard_map/slice | solution.py:86
  212.9 7.5 %collective-permute-start.5 = (bf16[9,5,1,256]{3,2,1,0:T(2,128)(2,1)S(1)}, bf16[9,5,1,256]{3,2,1,0:T(2,128)(2,1)S(1)}, u32[]{:S(2)}, u32[]{:S(2)}) collective-permute-start(bf16[9,5,1,256]{3,2,1,0:T(2,128)(2,1)S(1)} %fusion.51), channel_id=1, source_target_pairs={{1,0},{2,1},{3,2},{5,4},{6,5},{7,6},{9,8},{10,9},{11,10},{13,12},{... | collective-permute-start | bytes 69128 | tf_op jit(solution)/shard_map/ppermute | solution.py:38
  220.4 2.3 fusion.47
  222.7 2.2 fusion.44
  226.9 10.5 %slice.184 = bf16[9,2,60,256]{3,2,1,0:T(8,128)(2,1)} slice(bf16[9,5,121,256]{3,2,1,0:T(8,128)(2,1)} %pad_maximum_fusion.1), slice={[0:9:1], [0:4:2], [1:121:2], [0:256:1]} | slice | bytes 1105920 | tf_op jit(solution)/shard_map/slice | solution.py:86
  237.4 10.1 %slice.198 = bf16[9,2,60,256]{3,2,1,0:T(8,128)(2,1)} slice(bf16[9,5,121,256]{3,2,1,0:T(8,128)(2,1)} %pad_maximum_fusion.1), slice={[0:9:1], [2:5:2], [2:121:2], [0:256:1]} | slice | bytes 1105920 | tf_op jit(solution)/shard_map/slice | solution.py:86
  247.5 10.1 %slice.196 = bf16[9,2,60,256]{3,2,1,0:T(8,128)(2,1)} slice(bf16[9,5,121,256]{3,2,1,0:T(8,128)(2,1)} %pad_maximum_fusion.1), slice={[0:9:1], [2:5:2], [1:121:2], [0:256:1]} | slice | bytes 1105920 | tf_op jit(solution)/shard_map/slice | solution.py:86
  257.6 6.0 %slice.192 = bf16[9,2,60,256]{3,2,1,0:T(8,128)(2,1)} slice(bf16[9,5,121,256]{3,2,1,0:T(8,128)(2,1)S(1)} %copy-done.2), slice={[0:9:1], [1:5:2], [2:121:2], [0:256:1]} | slice | bytes 1105920 | tf_op jit(solution)/shard_map/slice | solution.py:86
  263.6 5.9 %slice.190 = bf16[9,2,60,256]{3,2,1,0:T(8,128)(2,1)} slice(bf16[9,5,121,256]{3,2,1,0:T(8,128)(2,1)S(1)} %copy-done.2), slice={[0:9:1], [1:5:2], [1:121:2], [0:256:1]} | slice | bytes 1105920 | tf_op jit(solution)/shard_map/slice | solution.py:86
  (81 shorter events, 35.5 us)
Async XLA Ops:
  6.5 71.8 %all-gather.3.cloned.1.call-start = ((), (), s32[]{:S(2)}) async-start(), calls=%async_computation | async-start | bytes 1327104 | tf_op jit(solution)/shard_map/all_gather | solution.py:117
  7.3 175.3 %all-gather.5.cloned.1.call-start = ((), (), s32[]{:S(2)}) async-start(), calls=%async_computation.1 | async-start | bytes 1327104 | tf_op jit(solution)/shard_map/all_gather | solution.py:119
  9.4 28.8 %collective-permute-start = (bf16[9,1,120,256]{3,2,1,0:T(8,128)(2,1)S(1)}, bf16[9,1,120,256]{3,2,1,0:T(8,128)(2,1)}, u32[]{:S(2)}, u32[]{:S(2)}) collective-permute-start(bf16[9,1,120,256]{3,2,1,0:T(8,128)(2,1)S(1)} %get-tuple-element.9), channel_id=1, source_target_pairs={{0,4},{4,8},{8,12},{12,16},{16,20},{20,24},{24,28},{1,5},{5,9},{9,... | collective-permute-start | bytes 1658888 | tf_op jit(solution)/shard_map/ppermute | solution.py:26
  12.6 28.5 %collective-permute-start.1 = (bf16[9,1,120,256]{3,2,1,0:T(8,128)(2,1)}, bf16[9,1,120,256]{3,2,1,0:T(8,128)(2,1)}, u32[]{:S(2)}, u32[]{:S(2)}) collective-permute-start(bf16[9,1,120,256]{3,2,1,0:T(8,128)(2,1)} %get-tuple-element.10), channel_id=1, source_target_pairs={{4,0},{8,4},{12,8},{16,12},{20,16},{24,20},{28,24},{5,1},{9,5},{13... | collective-permute-start | bytes 1658888 | tf_op jit(solution)/shard_map/ppermute | solution.py:28
  39.3 7.6 %copy-start.12 = (bf16[32,768]{1,0:T(8,128)(2,1)S(1)}, bf16[32,768]{1,0:T(8,128)(2,1)}, u32[]{:S(2)}) copy-start(bf16[32,768]{1,0:T(8,128)(2,1)} %param.9) | copy-start | bytes 147460
  42.3 36.0 %collective-permute-start.2 = (bf16[9,6,1,256]{3,2,1,0:T(2,128)(2,1)S(1)}, bf16[9,6,1,256]{3,2,1,0:T(2,128)(2,1)S(1)}, u32[]{:S(2)}, u32[]{:S(2)}) collective-permute-start(bf16[9,6,1,256]{3,2,1,0:T(2,128)(2,1)S(1)} %get-tuple-element.6), channel_id=1, source_target_pairs={{0,1},{1,2},{2,3},{4,5},{5,6},{6,7},{8,9},{9,10},{10,11},{12,13},{... | collective-permute-start | bytes 82952 | tf_op jit(solution)/shard_map/ppermute | solution.py:26
  72.8 12.2 %collective-permute-start.3 = (bf16[9,6,1,256]{3,2,1,0:T(2,128)(2,1)S(1)}, bf16[9,6,1,256]{3,2,1,0:T(2,128)(2,1)S(1)}, u32[]{:S(2)}, u32[]{:S(2)}) collective-permute-start(bf16[9,6,1,256]{3,2,1,0:T(2,128)(2,1)S(1)} %get-tuple-element.5), channel_id=1, source_target_pairs={{1,0},{2,1},{3,2},{5,4},{6,5},{7,6},{9,8},{10,9},{11,10},{13,12},{... | collective-permute-start | bytes 82952 | tf_op jit(solution)/shard_map/ppermute | solution.py:28
  78.4 3.8 %copy-start.11 = (bf16[256,2304]{1,0:T(8,128)(2,1)S(1)}, bf16[256,2304]{1,0:T(8,128)(2,1)}, u32[]{:S(2)}) copy-start(bf16[256,2304]{1,0:T(8,128)(2,1)} %all-gather.3.cloned.1.call-done) | copy-start | bytes 3538948
  90.7 2.9 copy-start
  114.7 1.6 copy-start.1
  116.3 1.0 copy-start.10
  117.3 1.5 slice-start
  118.8 1.5 slice-start.1
  123.3 51.9 %copy-start.13 = (f32[256]{0:T(256)S(1)}, f32[256]{0:T(256)}, u32[]{:S(2)}) copy-start(f32[256]{0:T(256)} %param.12) | copy-start | bytes 3076
  123.3 51.9 %copy-start.14 = (f32[256]{0:T(256)S(1)}, f32[256]{0:T(256)}, u32[]{:S(2)}) copy-start(f32[256]{0:T(256)} %param.11) | copy-start | bytes 3076
  179.7 12.5 %collective-permute-start.4 = (bf16[9,1,120,256]{3,2,1,0:T(8,128)(2,1)}, bf16[9,1,120,256]{3,2,1,0:T(8,128)(2,1)S(1)}, u32[]{:S(2)}, u32[]{:S(2)}) collective-permute-start(bf16[9,1,120,256]{3,2,1,0:T(8,128)(2,1)} %slice.226), channel_id=1, source_target_pairs={{4,0},{8,4},{12,8},{16,12},{20,16},{24,20},{28,24},{5,1},{9,5},{13... | collective-permute-start | bytes 1658888 | tf_op jit(solution)/shard_map/ppermute | solution.py:38
  212.8 7.5 %copy-start.8 = (bf16[9,2,60,256]{3,2,1,0:T(8,128)(2,1)S(1)}, bf16[9,2,60,256]{3,2,1,0:T(8,128)(2,1)}, u32[]{:S(2)}) copy-start(bf16[9,2,60,256]{3,2,1,0:T(8,128)(2,1)} %slice.188) | copy-start | bytes 1658884
  212.9 12.0 %collective-permute-start.5 = (bf16[9,5,1,256]{3,2,1,0:T(2,128)(2,1)S(1)}, bf16[9,5,1,256]{3,2,1,0:T(2,128)(2,1)S(1)}, u32[]{:S(2)}, u32[]{:S(2)}) collective-permute-start(bf16[9,5,1,256]{3,2,1,0:T(2,128)(2,1)S(1)} %fusion.51), channel_id=1, source_target_pairs={{1,0},{2,1},{3,2},{5,4},{6,5},{7,6},{9,8},{10,9},{11,10},{13,12},{... | collective-permute-start | bytes 69128 | tf_op jit(solution)/shard_map/ppermute | solution.py:38
  226.9 30.7 %copy-start.2 = (bf16[9,5,121,256]{3,2,1,0:T(8,128)(2,1)S(1)}, bf16[9,5,121,256]{3,2,1,0:T(8,128)(2,1)}, u32[]{:S(2)}) copy-start(bf16[9,5,121,256]{3,2,1,0:T(8,128)(2,1)} %pad_maximum_fusion.1) | copy-start | bytes 8363524
  270.5 3.1 %copy-start.9 = (bf16[9,2,60,256]{3,2,1,0:T(8,128)(2,1)S(1)}, bf16[9,2,60,256]{3,2,1,0:T(8,128)(2,1)}, u32[]{:S(2)}) copy-start(bf16[9,2,60,256]{3,2,1,0:T(8,128)(2,1)} %slice.192) | copy-start | bytes 1658884
  270.5 4.3 %copy-start.7 = (bf16[9,2,60,256]{3,2,1,0:T(8,128)(2,1)S(1)}, bf16[9,2,60,256]{3,2,1,0:T(8,128)(2,1)}, u32[]{:S(2)}) copy-start(bf16[9,2,60,256]{3,2,1,0:T(8,128)(2,1)} %slice.190) | copy-start | bytes 1658884
  272.0 4.2 %copy-start.5 = (f32[9,2,60,256]{3,2,1,0:T(8,128)S(1)}, f32[9,2,60,256]{3,2,1,0:T(8,128)}, u32[]{:S(2)}) copy-start(f32[9,2,60,256]{3,2,1,0:T(8,128)} %fusion.48) | copy-start | bytes 3317764
  272.1 4.2 %copy-start.6 = (bf16[9,2,60,256]{3,2,1,0:T(8,128)(2,1)S(1)}, bf16[9,2,60,256]{3,2,1,0:T(8,128)(2,1)}, u32[]{:S(2)}) copy-start(bf16[9,2,60,256]{3,2,1,0:T(8,128)(2,1)} %slice.184) | copy-start | bytes 1658884
  274.8 2.6 copy-start.3
  274.8 2.6 copy-start.4
  274.8 2.6 copy-start.15
Sparse Core Ops, SparseCore 0:
  9.5 52.3 all-gather.2
  64.2 39.7 all-gather.4
